TPU v7x, 32 devices: a whole 2x2x4 slice. The times are simulated.
32 devices in a mesh: group: 2 (over x), tm: 16 (over z, y, core).
Axes of the slice: x: 2, y: 2, z: 4, core: 2. Of those that a mesh axis runs over, the one named last changes fastest.
Arguments:
- records: float32 [256, 262144], P('group', 'tm'), parts along dimension 0, may hold values from -6 to 6
- labels: int32 [256], P('group'), parts along dimension 0, may hold values from 0 to 1
- first_weight: bfloat16 [131072, 1024], P('tm'), may hold values from -0.015625 to 0.015625
- first_bias: float32 [1024], replicated, may hold values from -3 to 3
- second_weight: float32 [1024], replicated, may hold values from -0.1875 to 0.1875
- second_bias: float32 [1], replicated, may hold values from -3 to 3
Outputs:
- loss: float32 [2], P('group'), parts along dimension 0
- grad_first: float32 [262144, 1024], P(('group', 'tm')), parts along dimension 0
- grad_bias: float32 [2048], P('group'), parts along dimension 0
- grad_second: float32 [2048], P('group'), parts along dimension 0
- grad_out_bias: float32 [2], P('group'), parts along dimension 0
There are 2 independent parts, one for each index of `group`. A program takes and returns all parts, laid end to end along the dimension named above; an argument that names none is the same for every part. Nothing has to cross between parts.
All inputs are finite; a program needn't handle non-finite values.
Results may differ from a plain program's by a relative error of at most 0.0079.
Values may be sent and summed in bfloat16 or wider, within the bound.
No kernel may reach another device: no remote copies, remote signals or barrier semaphores. Data moves between devices by JAX's collectives and lax.ppermute only.
A program may use at most 192 MiB of HBM per device.

v0:
```python
import math
import jax
import jax.numpy as jnp
from jax import lax
from jax.sharding import PartitionSpec as P

N1 = 512
N2 = 512


def first_table(count):
    rows = jnp.arange(count, dtype=jnp.int32)[:, None]
    cols = jnp.arange(count, dtype=jnp.int32)[None, :]
    angle = 2.0 * math.pi / count * (rows * cols % count).astype(jnp.float32)
    scale = 1.0 / math.sqrt(count)
    return jnp.concatenate([jnp.cos(angle) * scale, -jnp.sin(angle) * scale], 0).astype(
        jnp.bfloat16
    )


def second_table(count):
    rows = jnp.arange(count, dtype=jnp.int32)[:, None]
    cols = jnp.arange(count // 2, dtype=jnp.int32)[None, :]
    angle = 2.0 * math.pi / count * (rows * cols % count).astype(jnp.float32)
    scale = 1.0 / math.sqrt(count)
    cosine = jnp.cos(angle) * scale
    sine = jnp.sin(angle) * scale
    upper = jnp.concatenate([cosine, -sine], 1)
    lower = jnp.concatenate([sine, cosine], 1)
    return jnp.concatenate([upper, lower], 0).astype(jnp.bfloat16)


def on_device(records, labels, first_weight, first_bias, second_weight, second_bias):
    devices = lax.axis_size("tm")
    slow_rows = N2 // devices
    fast_cols = N1 // devices
    table_one = first_table(N2)
    table_two = second_table(N1)
    total_len = N1 * N2
    count_rec = records.shape[0]
    samples = records.astype(jnp.bfloat16).reshape(count_rec, slow_rows, N1)
    samples = jnp.transpose(samples, (0, 2, 1))
    partial_value = jnp.einsum(
        "rcn,kn->rck",
        lax.all_to_all(samples, "tm", split_axis=1, concat_axis=2, tiled=True),
        table_one,
        preferred_element_type=jnp.float32,
    )
    real_part = partial_value[:, :, :N2]
    imag_part = partial_value[:, :, N2:]
    fast = lax.axis_index("tm") * fast_cols + jnp.arange(fast_cols, dtype=jnp.int32)
    slow = jnp.arange(N2, dtype=jnp.int32)
    phase = (
        2.0 * math.pi / total_len * (fast[:, None] * slow[None, :] % total_len).astype(jnp.float32)
    )
    cosine = jnp.cos(phase)[None]
    sine = jnp.sin(phase)[None]
    twisted_re = real_part * cosine + imag_part * sine
    twisted_im = imag_part * cosine - real_part * sine
    stacked = jnp.stack([twisted_re, twisted_im], 1).astype(jnp.bfloat16)
    twisted = jnp.transpose(stacked, (0, 3, 1, 2))
    block = lax.all_to_all(twisted, "tm", split_axis=1, concat_axis=3, tiled=True)
    count = block.shape[0]
    joined = block.reshape(count, block.shape[1], 2 * N1)
    bins = jnp.einsum("rbm,mf->rbf", joined, table_two, preferred_element_type=jnp.float32)
    power = bins[:, :, : N1 // 2] ** 2 + bins[:, :, N1 // 2 :] ** 2
    features = jnp.log(1.0 + power).astype(jnp.bfloat16).reshape(count, block.shape[1] * (N1 // 2))
    target = labels.astype(jnp.float32)
    partial_sums = jnp.dot(features, first_weight, preferred_element_type=jnp.float32)
    pre = lax.psum(partial_sums, "tm") + first_bias[None, :]
    gate = jax.nn.sigmoid(pre)
    hidden = pre * gate
    logit = jnp.sum(hidden * second_weight[None, :], 1) + second_bias[0]
    dlogit = jax.nn.sigmoid(logit) - target
    dpre = (dlogit[:, None] * second_weight[None, :] * gate * (1.0 + pre * (1.0 - gate))).astype(
        jnp.bfloat16
    )
    grad_first = lax.dot_general(
        features, dpre, (((0,), (0,)), ((), ())), preferred_element_type=jnp.float32
    )
    grad_bias = jnp.sum(dpre.astype(jnp.float32), 0)
    grad_second = jnp.sum(hidden * dlogit[:, None], 0)
    loss = jnp.mean(jnp.log(1.0 + jnp.exp(logit)) - target * logit).reshape(1)
    grad_out_bias = jnp.sum(dlogit).reshape(1)
    return (loss, grad_first, grad_bias, grad_second, grad_out_bias)


def solution(mesh):
    return jax.shard_map(
        on_device,
        mesh=mesh,
        in_specs=(P("group", "tm"), P("group"), P("tm", None), P(), P(), P()),
        out_specs=(P("group"), P(("group", "tm"), None), P("group"), P("group"), P("group")),
        check_vma=False,
    )
```

profile of v0, /device:TPU:1, one launch (start us, length us, event | category | flops | bytes accessed | tf_op | source)
XLA Modules:
  0.0 488.0 jit_solution(15323579355672855773)
XLA Ops:
  7.2 7.2 %copy.31 = bf16[128,16384]{0,1:T(8,128)(2,1)} copy(f32[128,16384]{1,0:T(8,128)} %param.6) | data formatting | bytes 12582912 | tf_op args[0]
  14.4 6.9 %copy.32 = bf16[128,512,32]{0,2,1:T(8,128)(2,1)} copy(bf16[128,512,32]{0,1,2:T(8,128)(2,1)} %bitcast.39) | data formatting | bytes 8388608 | tf_op jit(solution)/shard_map/transpose | solution.py:42
  21.2 7.3 %all-to-all-start = ((bf16[128,512,32]{0,2,1:T(8,128)(2,1)}), bf16[128,512,32]{0,2,1:T(8,128)(2,1)}, u32[]{:S(2)}, u32[]{:S(2)}) async-start(bf16[128,512,32]{0,2,1:T(8,128)(2,1)} %copy.32), calls=%async_computation | async-start | bytes 8388608 | tf_op jit(solution)/shard_map/all_to_all | solution.py:45
  28.6 4.4 multiply_convert_fusion
  33.0 0.3 fusion.36
  33.3 73.3 %all-to-all-done = bf16[128,512,32]{0,2,1:T(8,128)(2,1)} async-done(((bf16[128,512,32]{0,2,1:T(8,128)(2,1)}), bf16[128,512,32]{0,2,1:T(8,128)(2,1)}, u32[]{:S(2)}, u32[]{:S(2)}) %all-to-all-start) | async-done | bytes 4194336 | tf_op jit(solution)/shard_map/all_to_all | solution.py:45
  106.7 3.4 copy.33
  110.1 4.5 convolution_bitcast_fusion
  114.7 5.8 %fusion = (bf16[128,1,32,512]{0,3,2,1:T(8,128)(2,1)S(1)}, bf16[128,1,32,512]{0,3,2,1:T(8,128)(2,1)}) fusion(f32[128,32,1024]{0,2,1:T(8,128)S(1)} %convolution_bitcast_fusion, f32[32,512]{1,0:T(8,128)S(1)} %get-tuple-element.14, f32[32,512]{1,0:T(8,128)S(1)} %get-tuple-element.13), kind=kLoop, calls=%fused_computation.4 | loop fusion | flops 16777216 | bytes 25296896 | tf_op jit(solution)/shard_map/stack | solution.py:60
  120.5 6.3 %maximum_bitcast_fusion = bf16[128,512,2,32]{0,1,3,2:T(8,128)(2,1)} fusion(bf16[128,1,32,512]{0,3,2,1:T(8,128)(2,1)} %get-tuple-element.10, bf16[128,1,32,512]{0,3,2,1:T(8,128)(2,1)S(1)} %get-tuple-element.9), kind=kLoop, calls=%fused_computation.1 | loop fusion | flops 4194304 | bytes 16777216 | tf_op jit(solution)/shard_map/transpose | solution.py:61
  126.8 12.0 %copy.35 = bf16[128,512,2,32]{0,3,2,1:T(8,128)(2,1)} copy(bf16[128,512,2,32]{0,1,3,2:T(8,128)(2,1)} %maximum_bitcast_fusion) | data formatting | bytes 16777216 | tf_op jit(solution)/shard_map/transpose | solution.py:61
  138.8 19.3 %all-to-all-start.1 = ((bf16[128,512,2,32]{0,3,2,1:T(8,128)(2,1)}), bf16[128,512,2,32]{0,3,2,1:T(8,128)(2,1)}, u32[]{:S(2)}, u32[]{:S(2)}) async-start(bf16[128,512,2,32]{0,3,2,1:T(8,128)(2,1)} %copy.35), calls=%async_computation.1 | async-start | bytes 16777216 | tf_op jit(solution)/shard_map/all_to_all | solution.py:62
  158.1 0.0 all-reduce.2.cloned.1.call-start
  158.2 2.2 fusion.28
  160.4 2.2 negate_convert_fusion
  162.6 146.6 %all-to-all-done.1 = bf16[128,512,2,32]{0,3,2,1:T(8,128)(2,1)} async-done(((bf16[128,512,2,32]{0,3,2,1:T(8,128)(2,1)}), bf16[128,512,2,32]{0,3,2,1:T(8,128)(2,1)}, u32[]{:S(2)}, u32[]{:S(2)}) %all-to-all-start.1) | async-done | bytes 8388640 | tf_op jit(solution)/shard_map/all_to_all | solution.py:62
  309.2 9.0 %copy.36 = bf16[128,32,2,16,32]{0,4,3,2,1:T(8,128)(2,1)} copy(bf16[128,32,2,16,32]{0,4,2,1,3:T(8,128)(2,1)} %bitcast.11) | data formatting | bytes 16777216 | tf_op jit(solution)/shard_map/all_to_all | solution.py:62
  318.2 7.0 %fusion.11 = f32[128,32,512]{2,0,1:T(8,128)S(1)} fusion(bf16[128,32,1024]{0,2,1:T(8,128)(2,1)} %bitcast.36, bf16[512,256]{1,0:T(8,128)(2,1)S(1)} %get-tuple-element.18, bf16[512,256]{1,0:T(8,128)(2,1)S(1)} %fusion.28, bf16[512,256]{1,0:T(8,128)(2,1)S(1)} %get-tuple-element.17), kind=kOutput, calls=%fused_computation.22 | convolution fusion | flops 4299161600 | bytes 17563648 | tf_op jit(solution)/shard_map/rbm,mf->rbf/dot_general | solution.py:65
  325.2 2.3 fusion.5
  327.5 3.2 copy.38
  330.7 0.0 copy-start
  330.7 0.0 copy-start.1
  330.7 0.0 copy-start.2
  330.7 8.9 %fusion.40 = f32[128,1024]{1,0:T(8,128)} fusion(bf16[128,8192]{0,1:T(8,128)(2,1)S(1)} %bitcast.37, bf16[8192,1024]{1,0:T(8,128)(2,1)} %param.8), kind=kOutput, calls=%fused_computation.70 | convolution fusion | flops 2147483648 | bytes 19398656 | tf_op jit(solution)/shard_map/dot_general | solution.py:69
  339.7 0.0 all-reduce.2.cloned.1.call-update
  340.3 121.1 %all-reduce.2.cloned.1.call-done = f32[128,1024]{1,0:T(8,128)} async-done(((f32[128,1024]{1,0:T(8,128)}), f32[128,1024]{1,0:T(8,128)}) %all-reduce.2.cloned.1.call-update) | async-done | bytes 524304 | tf_op jit(solution)/shard_map/psum | solution.py:70
  461.4 0.0 copy-done
  461.4 0.0 copy-done.1
  461.4 1.3 multiply_reduce_fusion.1
  462.7 0.0 copy-done.2
  462.7 0.7 fusion.39
  463.4 1.9 convert_reduce_fusion
  465.4 14.0 %fusion.41 = f32[8192,1024]{1,0:T(8,128)} fusion(bf16[128,8192]{0,1:T(8,128)(2,1)S(1)} %bitcast.38, bf16[128,1024]{1,0:T(8,128)(2,1)S(1)} %get-tuple-element.8), kind=kOutput, calls=%fused_computation.71 | convolution fusion | flops 2147483648 | bytes 35913728 | tf_op jit(solution)/shard_map/dot_general | solution.py:78
  (1 shorter events, 0.0 us)
Async XLA Ops:
  21.2 85.4 %all-to-all-start = ((bf16[128,512,32]{0,2,1:T(8,128)(2,1)}), bf16[128,512,32]{0,2,1:T(8,128)(2,1)}, u32[]{:S(2)}, u32[]{:S(2)}) async-start(bf16[128,512,32]{0,2,1:T(8,128)(2,1)} %copy.32), calls=%async_computation | async-start | bytes 8388608 | tf_op jit(solution)/shard_map/all_to_all | solution.py:45
  138.8 170.4 %all-to-all-start.1 = ((bf16[128,512,2,32]{0,3,2,1:T(8,128)(2,1)}), bf16[128,512,2,32]{0,3,2,1:T(8,128)(2,1)}, u32[]{:S(2)}, u32[]{:S(2)}) async-start(bf16[128,512,2,32]{0,3,2,1:T(8,128)(2,1)} %copy.35), calls=%async_computation.1 | async-start | bytes 16777216 | tf_op jit(solution)/shard_map/all_to_all | solution.py:62
  158.1 303.3 %all-reduce.2.cloned.1.call-start = ((), (), s32[]{:S(2)}) async-start(), calls=%async_computation.2 | async-start | bytes 1048576 | tf_op jit(solution)/shard_map/psum | solution.py:70
  330.7 130.7 %copy-start = (f32[1024]{0:T(1024)S(1)}, f32[1024]{0:T(1024)}, u32[]{:S(2)}) copy-start(f32[1024]{0:T(1024)} %param.10) | copy-start | bytes 12292
  330.7 130.7 %copy-start.1 = (f32[1024]{0:T(1024)S(1)}, f32[1024]{0:T(1024)}, u32[]{:S(2)}) copy-start(f32[1024]{0:T(1024)} %param.9) | copy-start | bytes 12292
  330.7 132.0 %copy-start.2 = (s32[128]{0:T(128)S(1)}, s32[128]{0:T(128)}, u32[]{:S(2)}) copy-start(s32[128]{0:T(128)} %param.7) | copy-start | bytes 1540
Sparse Core Ops, SparseCore 0:
  339.8 121.5 all-reduce.1
where the time goes:
time: 489 us; the launch traced here: 488 us
  waiting for transfers between devices  341 us (70%)
  local copies, waits for them, and re-layouts  41.7 us (9%)
  matrix products  34.5 us (7%)
  other arithmetic  27.5 us (6%)
  starting transfers between devices  26.7 us (5%)
  between operations  16.6 us (3%)
    all_to_all x1, waiting for transfers between devices, on_device(): lax.all_to_all(twisted, 'tm', split_axis=1, concat_axis=3, tiled=True)  147 us
    psum x1, waiting for transfers between devices, on_device(): pre = lax.psum(partial_sums, 'tm') + first_bias[None, :]  121 us
    all_to_all x1, waiting for transfers between devices, on_device(): lax.all_to_all(samples, 'tm', split_axis=1, concat_axis=2, tiled=True)  73.3 us
    all_to_all x1, starting transfers between devices, on_device(): lax.all_to_all(twisted, 'tm', split_axis=1, concat_axis=3, tiled=True)  19.3 us
    dot_general x1, matrix products, on_device(): lax.dot_general(features, dpre, (((0,), (0,)), ((), ())), preferred_eleme...  14 us
    transpose x1, local copies, waits for them, and re-layouts, on_device(): twisted = jnp.transpose(stacked, (0, 3, 1, 2))  12 us
  transfers between devices with their start and end apart: 3, of which 3 were waited for; matrix products, arithmetic and copies ran while one was open for 2% of the time, Pallas kernels for 0%

commit v1 on v0

--- a/solution.py
+++ b/solution.py
@@ -59,7 +59,12 @@
     twisted_im = imag_part * cosine - real_part * sine
     stacked = jnp.stack([twisted_re, twisted_im], 1).astype(jnp.bfloat16)
     twisted = jnp.transpose(stacked, (0, 3, 1, 2))
-    block = lax.all_to_all(twisted, "tm", split_axis=1, concat_axis=3, tiled=True)
+    block = jnp.concatenate(
+        lax.all_to_all(
+            jnp.stack(jnp.split(twisted, lax.axis_size("tm"), axis=1), axis=0), "tm", 0, 0
+        ),
+        axis=3,
+    )
     count = block.shape[0]
     joined = block.reshape(count, block.shape[1], 2 * N1)
     bins = jnp.einsum("rbm,mf->rbf", joined, table_two, preferred_element_type=jnp.float32)

time: 489 us -> 509 us (1.041)
  local copies, waits for them, and re-layouts: 41.7 us -> 61.1 us
    unnamed x7 -> x22, local copies, waits for them, and re-layouts: 7.25 us -> 35.7 us
    transpose x1 -> x0, local copies, waits for them, and re-layouts: 12 us -> none  [on_device(): twisted = jnp.transpose(stacked, (0, 3, 1, 2))]
    reshape x0 -> x1, local copies, waits for them, and re-layouts: none -> 10 us  [on_device(): jnp.concatenate(lax.all_to_all(jnp.stack(jnp.split(twisted, lax.axis_size...]
    all_to_all x1 -> x0, local copies, waits for them, and re-layouts: 8.97 us -> none  [on_device(): lax.all_to_all(twisted, 'tm', split_axis=1, concat_axis=3, tiled=True)]
where the time goes in v1:
time: 509 us; the launch traced here: 507 us
  waiting for transfers between devices  341 us (67%)
  local copies, waits for them, and re-layouts  61.1 us (12%)
  matrix products  34.5 us (7%)
  other arithmetic  27.3 us (5%)
  starting transfers between devices  26.9 us (5%)
  between operations  16.6 us (3%)
    all_to_all x1, waiting for transfers between devices, on_device(): lax.all_to_all(jnp.stack(jnp.split(twisted, lax.axis_size('tm'), axis=1),...  147 us
    psum x1, waiting for transfers between devices, on_device(): pre = lax.psum(partial_sums, 'tm') + first_bias[None, :]  121 us
    all_to_all x1, waiting for transfers between devices, on_device(): lax.all_to_all(samples, 'tm', split_axis=1, concat_axis=2, tiled=True)  73.3 us
    unnamed x22, local copies, waits for them, and re-layouts  35.7 us
    all_to_all x1, starting transfers between devices, on_device(): lax.all_to_all(jnp.stack(jnp.split(twisted, lax.axis_size('tm'), axis=1),...  19.3 us
    dot_general x1, matrix products, on_device(): lax.dot_general(features, dpre, (((0,), (0,)), ((), ())), preferred_eleme...  14 us
  transfers between devices with their start and end apart: 3, of which 3 were waited for; matrix products, arithmetic and copies ran while one was open for 2% of the time, Pallas kernels for 0%

profile of v1, /device:TPU:1, one launch (start us, length us, event | category | flops | bytes accessed | tf_op | source)
XLA Modules:
  0.0 507.4 jit_solution(13351568037099463998)
XLA Ops:
  7.2 7.2 %copy.23 = bf16[128,16384]{0,1:T(8,128)(2,1)} copy(f32[128,16384]{1,0:T(8,128)} %param.6) | data formatting | bytes 12582912 | tf_op args[0]
  14.4 6.9 %copy.24 = bf16[128,512,32]{0,2,1:T(8,128)(2,1)} copy(bf16[128,512,32]{0,1,2:T(8,128)(2,1)} %bitcast.101) | data formatting | bytes 8388608 | tf_op jit(solution)/shard_map/transpose | solution.py:42
  21.2 7.3 %all-to-all-start = ((bf16[128,512,32]{0,2,1:T(8,128)(2,1)}), bf16[128,512,32]{0,2,1:T(8,128)(2,1)}, u32[]{:S(2)}, u32[]{:S(2)}) async-start(bf16[128,512,32]{0,2,1:T(8,128)(2,1)} %copy.24), calls=%async_computation | async-start | bytes 8388608 | tf_op jit(solution)/shard_map/all_to_all | solution.py:45
  28.6 4.4 multiply_convert_fusion
  33.0 0.3 fusion.52
  33.3 73.3 %all-to-all-done = bf16[128,512,32]{0,2,1:T(8,128)(2,1)} async-done(((bf16[128,512,32]{0,2,1:T(8,128)(2,1)}), bf16[128,512,32]{0,2,1:T(8,128)(2,1)}, u32[]{:S(2)}, u32[]{:S(2)}) %all-to-all-start) | async-done | bytes 4194336 | tf_op jit(solution)/shard_map/all_to_all | solution.py:45
  106.7 3.4 copy.25
  110.1 4.5 convolution_bitcast_fusion
  114.7 5.8 %fusion = (bf16[128,1,32,512]{0,3,2,1:T(8,128)(2,1)S(1)}, bf16[128,1,32,512]{0,3,2,1:T(8,128)(2,1)}) fusion(f32[128,32,1024]{0,2,1:T(8,128)S(1)} %convolution_bitcast_fusion, f32[32,512]{1,0:T(8,128)S(1)} %get-tuple-element.14, f32[32,512]{1,0:T(8,128)S(1)} %get-tuple-element.13), kind=kLoop, calls=%fused_computation.4 | loop fusion | flops 16777216 | bytes 25296896 | tf_op jit(solution)/shard_map/stack | solution.py:60
  120.5 6.3 %maximum_bitcast_fusion = bf16[128,512,2,32]{0,1,3,2:T(8,128)(2,1)} fusion(bf16[128,1,32,512]{0,3,2,1:T(8,128)(2,1)} %get-tuple-element.10, bf16[128,1,32,512]{0,3,2,1:T(8,128)(2,1)S(1)} %get-tuple-element.9), kind=kLoop, calls=%fused_computation.1 | loop fusion | flops 4194304 | bytes 16777216 | tf_op jit(solution)/shard_map/transpose | solution.py:61
  126.8 1.9 fusion.39
  128.8 2.0 fusion.38
  130.7 1.9 fusion.37
  132.6 1.9 fusion.36
  134.5 1.9 fusion.35
  136.4 1.9 fusion.34
  138.3 1.9 fusion.33
  140.2 1.9 fusion.32
  142.0 1.9 fusion.31
  144.0 1.9 fusion.30
  145.9 1.9 fusion.29
  147.7 1.9 fusion.28
  149.6 1.9 fusion.27
  151.5 1.9 fusion.26
  153.4 1.9 fusion.25
  155.3 1.9 fusion.24
  157.2 19.3 %all-to-all-start.1 = ((bf16[16,128,32,2,32]{1,2,4,3,0:T(8,128)(2,1)}), bf16[16,128,32,2,32]{1,2,4,3,0:T(8,128)(2,1)}, u32[]{:S(2)}, u32[]{:S(2)}) async-start(bf16[16,128,32,2,32]{1,2,4,3,0:T(8,128)(2,1)} %fusion.24), calls=%async_computation.1 | async-start | bytes 16777216 | tf_op jit(solution)/shard_map/all_to_all | solution.py:63
  176.5 0.2 all-reduce.2.cloned.1.call-start
  176.7 2.0 fusion.44
  178.7 2.2 negate_convert_fusion
  180.9 146.7 %all-to-all-done.1 = bf16[16,128,32,2,32]{1,2,4,3,0:T(8,128)(2,1)} async-done(((bf16[16,128,32,2,32]{1,2,4,3,0:T(8,128)(2,1)}), bf16[16,128,32,2,32]{1,2,4,3,0:T(8,128)(2,1)}, u32[]{:S(2)}, u32[]{:S(2)}) %all-to-all-start.1) | async-done | bytes 8388640 | tf_op jit(solution)/shard_map/all_to_all | solution.py:63
  327.6 10.0 %copy.27 = bf16[128,32,2,16,32]{0,4,3,2,1:T(8,128)(2,1)} copy(bf16[128,32,2,16,32]{0,1,4,2,3:T(8,128)(2,1)} %bitcast.26) | data formatting | bytes 16777216 | tf_op jit(solution)/shard_map/reshape | solution.py:62
  337.6 7.0 %fusion.11 = f32[128,32,512]{2,0,1:T(8,128)S(1)} fusion(bf16[128,32,1024]{0,2,1:T(8,128)(2,1)} %bitcast.98, bf16[512,256]{1,0:T(8,128)(2,1)S(1)} %get-tuple-element.18, bf16[512,256]{1,0:T(8,128)(2,1)S(1)} %fusion.44, bf16[512,256]{1,0:T(8,128)(2,1)S(1)} %get-tuple-element.17), kind=kOutput, calls=%fused_computation.22 | convolution fusion | flops 4299161600 | bytes 17563648 | tf_op jit(solution)/shard_map/rbm,mf->rbf/dot_general | solution.py:70
  344.6 2.3 fusion.5
  346.9 3.2 copy.29
  350.1 0.0 copy-start
  350.1 0.0 copy-start.1
  350.1 0.0 copy-start.2
  350.1 8.9 %fusion.56 = f32[128,1024]{1,0:T(8,128)} fusion(bf16[128,8192]{0,1:T(8,128)(2,1)S(1)} %bitcast.99, bf16[8192,1024]{1,0:T(8,128)(2,1)} %param.8), kind=kOutput, calls=%fused_computation.102 | convolution fusion | flops 2147483648 | bytes 19398656 | tf_op jit(solution)/shard_map/dot_general | solution.py:74
  359.1 0.0 all-reduce.2.cloned.1.call-update
  359.7 121.1 %all-reduce.2.cloned.1.call-done = f32[128,1024]{1,0:T(8,128)} async-done(((f32[128,1024]{1,0:T(8,128)}), f32[128,1024]{1,0:T(8,128)}) %all-reduce.2.cloned.1.call-update) | async-done | bytes 524304 | tf_op jit(solution)/shard_map/psum | solution.py:75
  480.8 0.0 copy-done
  480.8 0.0 copy-done.1
  480.8 1.3 multiply_reduce_fusion.1
  482.1 0.0 copy-done.2
  482.1 0.7 fusion.55
  482.8 1.9 convert_reduce_fusion
  484.7 14.0 %fusion.57 = f32[8192,1024]{1,0:T(8,128)} fusion(bf16[128,8192]{0,1:T(8,128)(2,1)S(1)} %bitcast.100, bf16[128,1024]{1,0:T(8,128)(2,1)S(1)} %get-tuple-element.8), kind=kOutput, calls=%fused_computation.103 | convolution fusion | flops 2147483648 | bytes 35913728 | tf_op jit(solution)/shard_map/dot_general | solution.py:83
  (1 shorter events, 0.0 us)
Async XLA Ops:
  21.2 85.4 %all-to-all-start = ((bf16[128,512,32]{0,2,1:T(8,128)(2,1)}), bf16[128,512,32]{0,2,1:T(8,128)(2,1)}, u32[]{:S(2)}, u32[]{:S(2)}) async-start(bf16[128,512,32]{0,2,1:T(8,128)(2,1)} %copy.24), calls=%async_computation | async-start | bytes 8388608 | tf_op jit(solution)/shard_map/all_to_all | solution.py:45
  157.2 170.4 %all-to-all-start.1 = ((bf16[16,128,32,2,32]{1,2,4,3,0:T(8,128)(2,1)}), bf16[16,128,32,2,32]{1,2,4,3,0:T(8,128)(2,1)}, u32[]{:S(2)}, u32[]{:S(2)}) async-start(bf16[16,128,32,2,32]{1,2,4,3,0:T(8,128)(2,1)} %fusion.24), calls=%async_computation.1 | async-start | bytes 16777216 | tf_op jit(solution)/shard_map/all_to_all | solution.py:63
  176.5 304.4 %all-reduce.2.cloned.1.call-start = ((), (), s32[]{:S(2)}) async-start(), calls=%async_computation.2 | async-start | bytes 1048576 | tf_op jit(solution)/shard_map/psum | solution.py:75
  350.1 130.7 %copy-start = (f32[1024]{0:T(1024)S(1)}, f32[1024]{0:T(1024)}, u32[]{:S(2)}) copy-start(f32[1024]{0:T(1024)} %param.10) | copy-start | bytes 12292
  350.1 130.7 %copy-start.1 = (f32[1024]{0:T(1024)S(1)}, f32[1024]{0:T(1024)}, u32[]{:S(2)}) copy-start(f32[1024]{0:T(1024)} %param.9) | copy-start | bytes 12292
  350.1 132.0 %copy-start.2 = (s32[128]{0:T(128)S(1)}, s32[128]{0:T(128)}, u32[]{:S(2)}) copy-start(s32[128]{0:T(128)} %param.7) | copy-start | bytes 1540
Sparse Core Ops, SparseCore 0:
  359.2 121.5 all-reduce.1
